TPU v7x, 128 devices: a whole 4x4x4 slice. The times are simulated.
128 devices in a mesh: dp: 8 (over z, y_hi), fsdp: 16 (over y_lo, x, core).
Axes of the slice: x: 4, y: 4 (y_hi: 2, y_lo: 2; y = y_hi * 2 + y_lo), z: 4, core: 2. Of those that a mesh axis runs over, the one named last changes fastest.
Arguments:
- tokens: bfloat16 [16, 1024, 2048], P('dp', 'fsdp'), may hold values from -6 to 6
- w_qkv: bfloat16 [2048, 3072], P('fsdp', 'dp'), may hold values from -0.1875 to 0.1875
- w_out: bfloat16 [1024, 2048], P('fsdp', 'dp'), may hold values from -0.375 to 0.375
- ln_gain: float32 [2048], replicated, may hold values from 0.5 to 1.5
- ln_bias: float32 [2048], replicated, may hold values from -3 to 3
- kv_pool: bfloat16 [64, 128, 2048], P('fsdp'), may hold values from -300 to 300
- page_table: int32 [4, 16], replicated, may hold values from 0 to 63, as said below
- prefix_len: int32 [4], replicated, may hold values from 1 to 2048, as said below
- group_of: int32 [16], P('dp'), may hold values from 0 to 3, as said below
Outputs:
- hidden_out: bfloat16 [16, 1024, 2048], P('dp', 'fsdp')
- new_cache: bfloat16 [16, 1024, 2048], P('dp', 'fsdp')
Inputs may be any that keep to these rules, and one draw needn't show every extreme that they name: `page_table`: a permutation of the pool's slots. `prefix_len`: some group's prefix is exactly 2048 long. `group_of`: each group has 4 requests.
All inputs are finite; a program needn't handle non-finite values.
Results may differ from a plain program's by a relative error of at most 0.012.
The roundings to bfloat16 on the way count: a program that leaves them out, or rounds other values in their place, can miss the bound.
Values may be sent and summed in bfloat16 or wider, within the bound.
A program may use at most 128 MiB of HBM per device.

v0:
```python
import math
import jax
import jax.numpy as jnp
from jax import lax
from jax.sharding import PartitionSpec as P

HD = 128
neg_big = -1e30
ln_eps = 1e-06


def attend_rows(
    queries, row_req, row_pos, row_group, row_len, key_rows, value_rows, key_req, key_pos, key_group
):
    row_count = queries.shape[0]
    heads = queries.shape[1]
    head_dim = queries.shape[2]
    block_rows = min(512, row_count)
    inv_root = 1.0 / math.sqrt(head_dim)

    def one_block(first_row):
        q_block = lax.dynamic_slice_in_dim(queries, first_row, block_rows, 0)
        req_block = lax.dynamic_slice_in_dim(row_req, first_row, block_rows, 0)
        pos_block = lax.dynamic_slice_in_dim(row_pos, first_row, block_rows, 0)
        group_block = lax.dynamic_slice_in_dim(row_group, first_row, block_rows, 0)
        len_block = lax.dynamic_slice_in_dim(row_len, first_row, block_rows, 0)
        scores = (
            jnp.einsum("nhd,khd->nhk", q_block, key_rows, preferred_element_type=jnp.float32)
            * inv_root
        )
        from_prefix = (key_group[None, :] == group_block[:, None]) & (
            key_pos[None, :] < len_block[:, None]
        )
        from_new = (key_req[None, :] == req_block[:, None]) & (
            key_pos[None, :] <= pos_block[:, None]
        )
        is_live = jnp.where(key_req[None, :] < 0, from_prefix, from_new)
        scores = jnp.where(is_live[:, None, :], scores, neg_big)
        row_max = jnp.max(scores, axis=2)
        expo = jnp.where(is_live[:, None, :], jnp.exp(scores - row_max[:, :, None]), 0.0)
        row_total = jnp.sum(expo, axis=2)
        summed = jnp.einsum(
            "nhk,khd->nhd",
            expo.astype(jnp.bfloat16),
            value_rows,
            preferred_element_type=jnp.float32,
        )
        return (summed, row_max, row_total)

    starts = jnp.arange(row_count // block_rows, dtype=jnp.int32) * block_rows
    summed, row_max, row_total = lax.map(one_block, starts)
    return (
        summed.reshape(row_count, heads, head_dim),
        row_max.reshape(row_count, heads),
        row_total.reshape(row_count, heads),
    )


def body(tokens, w_qkv, w_out, ln_gain, ln_bias, kv_pool, page_table, prefix_len, group_of):
    req_count = tokens.shape[0]
    tok_count = tokens.shape[1]
    width = tokens.shape[2]
    owners = lax.axis_size("fsdp")
    owner_index = lax.axis_index("fsdp")
    inner = w_out.shape[0] * owners
    heads = inner // HD
    new_len = tok_count * owners
    flat_rows = tokens.reshape(req_count * tok_count, width)
    qkv_cols, out_cols = (
        lax.all_gather(w_qkv, "dp", axis=1, tiled=True),
        lax.all_gather(w_out, "dp", axis=1, tiled=True),
    )
    left_rows = flat_rows
    qkv_sum = jnp.dot(
        left_rows,
        lax.all_gather(qkv_cols, "fsdp", axis=0, tiled=True),
        preferred_element_type=jnp.float32,
    )
    qkv = qkv_sum.astype(jnp.bfloat16).reshape(req_count, tok_count, 3 * inner)
    own_queries = qkv[:, :, :inner]
    new_cache = qkv[:, :, inner:]
    own_keys = qkv[:, :, inner : 2 * inner]
    own_values = qkv[:, :, 2 * inner :]
    slot_count = kv_pool.shape[0]
    page_len = kv_pool.shape[1]
    group_count = page_table.shape[0]
    page_slots = page_table.shape[1]
    slot_ids = owner_index * slot_count + jnp.arange(slot_count, dtype=jnp.int32)
    matches = (page_table[:, :, None] == slot_ids[None, None, :]).astype(jnp.int32)
    slot_group = jnp.sum(
        matches * jnp.arange(group_count, dtype=jnp.int32)[:, None, None], axis=(0, 1)
    )
    slot_page = jnp.sum(
        matches * jnp.arange(page_slots, dtype=jnp.int32)[None, :, None], axis=(0, 1)
    )
    pool_pos = (
        slot_page[:, None] * page_len + jnp.arange(page_len, dtype=jnp.int32)[None, :]
    ).reshape(-1)
    pool_group = jnp.broadcast_to(slot_group[:, None], (slot_count, page_len)).reshape(-1)
    pool_req = jnp.full(pool_pos.shape, -1, jnp.int32)
    pool_keys = kv_pool[:, :, :inner].reshape(slot_count * page_len, heads, HD)
    pool_values = kv_pool[:, :, inner:].reshape(slot_count * page_len, heads, HD)
    member = (group_of[:, None] == jnp.arange(group_count, dtype=jnp.int32)[None, :]).astype(
        jnp.int32
    )
    request_len = jnp.sum(member * prefix_len[None, :], axis=1)

    def describe(row_positions):
        span_len = row_positions.shape[0]
        req_ids = jnp.broadcast_to(
            jnp.arange(req_count, dtype=jnp.int32)[:, None], (req_count, span_len)
        ).reshape(-1)
        pos_ids = jnp.broadcast_to(row_positions[None, :], (req_count, span_len)).reshape(-1)
        group_ids = jnp.broadcast_to(group_of[:, None], (req_count, span_len)).reshape(-1)
        len_ids = jnp.broadcast_to(request_len[:, None], (req_count, span_len)).reshape(-1)
        return (req_ids, pos_ids, group_ids, len_ids)

    all_positions = jnp.arange(new_len, dtype=jnp.int32)
    own_positions = owner_index * tok_count + jnp.arange(tok_count, dtype=jnp.int32)
    all_info = describe(all_positions)
    own_info = describe(own_positions)
    whole_q, whole_k, whole_v = (
        lax.all_gather(own_queries, "fsdp", axis=1, tiled=True),
        lax.all_gather(own_keys, "fsdp", axis=1, tiled=True),
        lax.all_gather(own_values, "fsdp", axis=1, tiled=True),
    )
    owner_sum, owner_max, owner_total = attend_rows(
        whole_q.reshape(req_count * new_len, heads, HD),
        all_info[0],
        all_info[1],
        all_info[2],
        all_info[3],
        pool_keys,
        pool_values,
        pool_req,
        pool_pos,
        pool_group,
    )
    owner_norm = (owner_sum / jnp.maximum(owner_total, 1.0)[:, :, None]).astype(jnp.bfloat16)
    part_norm = owner_norm.reshape(1, req_count, new_len, inner)
    part_max = owner_max.reshape(1, req_count, new_len, heads)
    part_total = owner_total.reshape(1, req_count, new_len, heads)
    got_norm = lax.all_to_all(part_norm, "fsdp", split_axis=2, concat_axis=0, tiled=True)
    got_max, got_total = (
        lax.all_to_all(part_max, "fsdp", split_axis=2, concat_axis=0, tiled=True),
        lax.all_to_all(part_total, "fsdp", split_axis=2, concat_axis=0, tiled=True),
    )
    local_sum, local_max, local_total = attend_rows(
        own_queries.reshape(req_count * tok_count, heads, HD),
        own_info[0],
        own_info[1],
        own_info[2],
        own_info[3],
        whole_k.reshape(req_count * new_len, heads, HD),
        whole_v.reshape(req_count * new_len, heads, HD),
        all_info[0],
        all_info[1],
        jnp.full(all_info[0].shape, -1, jnp.int32),
    )
    local_sum = local_sum.reshape(req_count, tok_count, heads, HD)
    local_max = local_max.reshape(req_count, tok_count, heads)
    local_total = local_total.reshape(req_count, tok_count, heads)
    overall = jnp.maximum(jnp.max(got_max, axis=0), local_max)
    factor = got_total * jnp.exp(got_max - overall[None])
    local_factor = jnp.exp(local_max - overall)
    part_count = got_norm.shape[0]
    normed_parts = got_norm.reshape(part_count, req_count, tok_count, heads, HD)
    numer = jnp.sum(normed_parts.astype(jnp.float32) * factor[..., None], axis=0)
    numer = numer + local_sum * local_factor[..., None]
    denom = jnp.sum(factor, axis=0) + local_total * local_factor
    attn = (numer / denom[..., None]).reshape(req_count * tok_count, inner).astype(jnp.bfloat16)
    left_rows = attn
    proj = jnp.dot(
        left_rows,
        lax.all_gather(out_cols, "fsdp", axis=0, tiled=True),
        preferred_element_type=jnp.float32,
    )
    mixed = flat_rows.astype(jnp.float32) + proj
    mean_row = jnp.mean(mixed, axis=1, keepdims=True)
    centred = mixed - mean_row
    var_row = jnp.mean(centred * centred, axis=1, keepdims=True)
    normed = centred * lax.rsqrt(var_row + ln_eps) * ln_gain[None, :] + ln_bias[None, :]
    hidden_out = normed.astype(jnp.bfloat16).reshape(req_count, tok_count, width)
    return (hidden_out, new_cache)


def solution(mesh):
    in_specs = (
        P("dp", "fsdp", None),
        P("fsdp", "dp"),
        P("fsdp", "dp"),
        P(),
        P(),
        P("fsdp", None, None),
        P(),
        P(),
        P("dp"),
    )
    out_specs = (P("dp", "fsdp", None), P("dp", "fsdp", None))
    return jax.shard_map(body, mesh=mesh, in_specs=in_specs, out_specs=out_specs, check_vma=False)
```

profile of v0, /device:TPU:3, one launch (start us, length us, event | category | flops | bytes accessed | tf_op | source)
XLA Modules:
  0.0 372.2 jit_solution(6619067220473818297)
XLA Ops:
  7.2 35.5 %all_gather.21 = bf16[128,3072]{1,0:T(8,128)(2,1)} all-gather(bf16[128,384]{1,0:T(8,128)(2,1)} %param.12), channel_id=1, replica_groups=mesh['dp'=8,'fsdp'=16] {'dp'}, dimensions={1}, use_global_device_ids=true | all-gather | bytes 884736 | tf_op jit(solution)/shard_map/all_gather | solution.py:70
  42.8 78.4 %all-gather.6.cloned.1.call-done = bf16[2048,3072]{1,0:T(8,128)(2,1)} async-done(((bf16[128,3072]{1,0:T(8,128)(2,1)}), bf16[2048,3072]{1,0:T(8,128)(2,1)}) %all-gather.6.cloned.1.call-update) | async-done | bytes 12582928 | tf_op jit(solution)/shard_map/all_gather | solution.py:76
  121.2 6.6 %convolution_convert_fusion = bf16[128,3072]{1,0:T(8,128)(2,1)S(1)} fusion(bf16[128,2048]{1,0:T(8,128)(2,1)} %bitcast.180, bf16[2048,3072]{1,0:T(8,128)(2,1)} %all-gather.6.cloned.1.call-done), kind=kOutput, calls=%fused_computation.42 | convolution fusion | flops 1611005952 | bytes 13893632 | tf_op jit(solution)/shard_map/dot_general | solution.py:74
  130.1 31.3 %all_gather.26 = bf16[64,2048]{1,0:T(8,128)(2,1)} all-gather(bf16[64,256]{1,0:T(8,128)(2,1)S(1)} %copy-done.2), channel_id=1, replica_groups=mesh['dp'=8,'fsdp'=16] {'dp'}, dimensions={1}, use_global_device_ids=true | all-gather | bytes 294912 | tf_op jit(solution)/shard_map/all_gather | solution.py:71
  167.5 5.2 %copy.131 = bf16[256,8,8,128]{3,2,1,0:T(8,128)(2,1)} copy(bf16[256,8,8,128]{3,1,2,0:T(8,128)(2,1)} %bitcast.169) | data formatting | bytes 8388608
  172.7 54.2 %while.4 = (s32[]{:T(128)}, f32[4,512,8,128]{3,2,1,0:T(8,128)}, f32[4,512,8]{1,2,0:T(8,128)S(1)}, f32[4,512,8]{1,2,0:T(8,128)S(1)}, s32[4]{0:T(128)S(1)}, /*inde...) while((s32[]{:T(128)}, f32[4,512,8,128]{3,2,1,0:T(8,128)}, ...), condition=%wide.region_6.7_spmd.clone, body=%wide.region_3.6_spmd.clone.sunk | while | flops 1101783552 | bytes 37900532 | solution.py:51
  205.8 3.0 fusion.65
  229.7 10.5 %all-to-all-start.2 = ((f32[16,1,1024]{2,1,0:T(1,128)}), f32[16,1,1024]{2,1,0:T(1,128)S(1)}, u32[]{:S(2)}, u32[]{:S(2)}) async-start(f32[16,1,1024]{2,1,0:T(1,128)} %reshape.384), calls=%async_computation.2 | async-start | bytes 131072 | tf_op jit(solution)/shard_map/all_to_all | solution.py:145
  243.0 9.3 %reshape.377 = f32[1,2,1024,1024]{3,2,1,0:T(8,128)} reshape(f32[4,512,8,128]{3,2,1,0:T(8,128)} %get-tuple-element.136) | data formatting | bytes 16777216 | tf_op jit(solution)/shard_map/reshape | solution.py:53
  252.6 6.4 %div.34 = f32[2048,8,128]{2,1,0:T(8,128)} broadcast(f32[2048,8]{1,0:T(8,128)S(1)} %copy.100), dimensions={0,1} | broadcast | bytes 8454144 | tf_op jit(solution)/shard_map/div | solution.py:139
  258.9 9.3 %div.35 = f32[1,2,1024,1024]{3,2,1,0:T(8,128)} reshape(f32[2048,8,128]{2,1,0:T(8,128)} %div.34) | data formatting | bytes 16777216 | tf_op jit(solution)/shard_map/div | solution.py:139
  268.3 5.7 %all-to-all-start.1 = ((f32[16,1,1024]{2,1,0:T(1,128)}), f32[16,1,1024]{2,1,0:T(1,128)S(1)}, u32[]{:S(2)}, u32[]{:S(2)}) async-start(f32[16,1,1024]{2,1,0:T(1,128)} %reshape.386), calls=%async_computation.1 | async-start | bytes 131072 | tf_op jit(solution)/shard_map/all_to_all | solution.py:146
  274.0 7.8 %divide_convert_fusion = bf16[1,2,1024,1024]{3,2,1,0:T(8,128)(2,1)S(1)} fusion(f32[1,2,1024,1024]{3,2,1,0:T(8,128)} %reshape.377, f32[1,2,1024,1024]{3,2,1,0:T(8,128)} %div.35), kind=kLoop, calls=%fused_computation.30 | loop fusion | flops 4194304 | bytes 20971520 | tf_op jit(solution)/shard_map/convert_element_type | solution.py:139
  281.8 6.2 %copy.101 = bf16[1,2,1024,1024]{3,1,0,2:T(2,128)(2,1)} copy(bf16[1,2,1024,1024]{3,2,1,0:T(8,128)(2,1)S(1)} %divide_convert_fusion) | data formatting | bytes 8388608 | tf_op jit(solution)/shard_map/convert_element_type | solution.py:139
  288.1 6.1 %all-to-all-start = ((bf16[1,2,1024,1024]{3,1,0,2:T(2,128)(2,1)}), bf16[1,2,1024,1024]{3,1,0,2:T(2,128)(2,1)}, u32[]{:S(2)}, u32[]{:S(2)}) async-start(bf16[1,2,1024,1024]{3,1,0,2:T(2,128)(2,1)} %copy.101), calls=%async_computation | async-start | bytes 8388608 | tf_op jit(solution)/shard_map/all_to_all | solution.py:143
  296.8 3.3 copy.136
  300.1 4.9 %fusion.22 = (f32[128,8]{0,1:T(8,128)S(1)}, f32[8,2048,128]{2,1,0:T(8,128)}) fusion(pred[128,2048]{0,1:T(8,128)(4,1)S(1)} %and_select_fusion, bf16[128,8,128]{2,1,0:T(8,128)(2,1)S(1)} %bitcast.189, bf16[2048,8,128]{2,1,0:T(8,128)(2,1)S(1)} %bitcast.170), kind=kOutput, calls=%fused_computation.31 | convolution fusion | flops 543161344 | bytes 13111296 | tf_op jit(solution)/shard_map/while/body/eval_jaxpr/nhd,khd->nhk/dot_general | solution.py:28
  305.1 4.5 %fusion.23 = f32[128,8]{0,1:T(8,128)S(1)} fusion(f32[8,2048,128]{2,1,0:T(8,128)} %get-tuple-element.280, f32[128,8]{0,1:T(8,128)S(1)} %get-tuple-element.279, pred[128,2048]{0,1:T(8,128)(4,1)S(1)} %and_select_fusion), kind=kLoop, calls=%fused_computation.32 | loop fusion | flops 10484736 | bytes 8658944 | tf_op jit(solution)/shard_map/while/body/eval_jaxpr/reduce_sum | solution.py:41
  309.6 3.3 copy.138
  312.9 5.7 %fusion.25 = f32[8,128,128]{2,1,0:T(8,128)S(1)} fusion(bf16[2048,8,128]{2,1,0:T(8,128)(2,1)S(1)} %bitcast.171, f32[8,2048,128]{2,1,0:T(8,128)} %get-tuple-element.280, f32[128,8]{0,1:T(8,128)S(1)} %get-tuple-element.279, pred[128,2048]{0,1:T(8,128)(4,1)S(1)} %and_select_fusion), kind=kOutput, calls=%fused_computation.34 | convolution fusion | flops 547356672 | bytes 13373440 | tf_op jit(solution)/shard_map/while/body/eval_jaxpr/nhk,khd->nhd/dot_general | solution.py:42
  326.0 4.6 %mul.121 = f32[16,2,64,8,128]{4,3,1,2,0:T(8,128)} broadcast(f32[16,2,64,8]{3,1,2,0:T(2,128)S(1)} %copy.109), dimensions={0,1,2,3} | broadcast | bytes 8454144 | tf_op jit(solution)/shard_map/mul | solution.py:168
  330.6 11.0 %mul.122 = f32[16,1,2,64,1024]{4,2,3,0,1:T(2,128)} reshape(f32[16,2,64,8,128]{4,3,1,2,0:T(8,128)} %mul.121) | data formatting | bytes 16777216 | tf_op jit(solution)/shard_map/mul | solution.py:168
  341.6 9.1 %all-to-all-done = bf16[1,2,1024,1024]{3,1,0,2:T(2,128)(2,1)} async-done(((bf16[1,2,1024,1024]{3,1,0,2:T(2,128)(2,1)}), bf16[1,2,1024,1024]{3,1,0,2:T(2,128)(2,1)}, u32[]{:S(2)}, u32[]{:S(2)}) %all-to-all-start) | async-done | bytes 4194336 | tf_op jit(solution)/shard_map/all_to_all | solution.py:143
  350.7 9.5 %fusion.21 = f32[2,64,1024]{2,0,1:T(2,128)S(1)} fusion(f32[16,1,2,64,1024]{4,2,3,0,1:T(2,128)} %mul.122, bf16[1,2,16,64,1024]{4,1,3,2,0:T(2,128)(2,1)} %bitcast.26), kind=kLoop, calls=%fused_computation.27 | loop fusion | flops 6160384 | bytes 13107200 | tf_op jit(solution)/shard_map/reduce_sum | solution.py:168
  (144 shorter events, 73.1 us)
Async XLA Ops:
  7.2 114.0 %all-gather.6.cloned.1.call-start = ((), (), s32[]{:S(2)}) async-start(), calls=%async_computation.3 | async-start | bytes 13369344 | tf_op jit(solution)/shard_map/all_gather | solution.py:76
  42.8 124.7 %all-gather.8.cloned.1.call-start = ((), (), s32[]{:S(2)}) async-start(), calls=%async_computation.4 | async-start | bytes 4456448 | tf_op jit(solution)/shard_map/all_gather | solution.py:123
  121.2 8.9 %copy-start.2 = (bf16[64,256]{1,0:T(8,128)(2,1)S(1)}, bf16[64,256]{1,0:T(8,128)(2,1)}, u32[]{:S(2)}) copy-start(bf16[64,256]{1,0:T(8,128)(2,1)} %param.13) | copy-start | bytes 98308
  121.2 40.3 %copy-start.6 = (s32[2]{0:T(128)S(1)}, s32[2]{0:T(128)}, u32[]{:S(2)}) copy-start(s32[2]{0:T(128)} %param.19) | copy-start | bytes 28
  121.2 40.4 %copy-start.5 = (s32[4,16]{1,0:T(4,128)S(1)}, s32[4,16]{1,0:T(4,128)}, u32[]{:S(2)}) copy-start(s32[4,16]{1,0:T(4,128)} %param.17) | copy-start | bytes 772
  121.2 40.6 %copy-start.7 = (s32[4]{0:T(128)S(1)}, s32[4]{0:T(128)}, u32[]{:S(2)}) copy-start(s32[4]{0:T(128)} %param.18) | copy-start | bytes 52
  128.7 168.1 %all-gather.10.cloned.1.call-start = ((), (), s32[]{:S(2)}) async-start(), calls=%async_computation.5 | async-start | bytes 4456448 | tf_op jit(solution)/shard_map/all_gather | solution.py:124
  129.5 180.1 %all-gather.12.cloned.1.call-start = ((), (), s32[]{:S(2)}) async-start(), calls=%async_computation.6 | async-start | bytes 4456448 | tf_op jit(solution)/shard_map/all_gather | solution.py:125
  130.0 231.1 %all-gather.14.cloned.1.call-start = ((), (), s32[]{:S(2)}) async-start(), calls=%async_computation.7 | async-start | bytes 4456448 | tf_op jit(solution)/shard_map/all_gather | solution.py:175
  229.7 38.5 %all-to-all-start.2 = ((f32[16,1,1024]{2,1,0:T(1,128)}), f32[16,1,1024]{2,1,0:T(1,128)S(1)}, u32[]{:S(2)}, u32[]{:S(2)}) async-start(f32[16,1,1024]{2,1,0:T(1,128)} %reshape.384), calls=%async_computation.2 | async-start | bytes 131072 | tf_op jit(solution)/shard_map/all_to_all | solution.py:145
  268.3 19.8 %all-to-all-start.1 = ((f32[16,1,1024]{2,1,0:T(1,128)}), f32[16,1,1024]{2,1,0:T(1,128)S(1)}, u32[]{:S(2)}, u32[]{:S(2)}) async-start(f32[16,1,1024]{2,1,0:T(1,128)} %reshape.386), calls=%async_computation.1 | async-start | bytes 131072 | tf_op jit(solution)/shard_map/all_to_all | solution.py:146
  281.8 15.0 %copy-start.1 = (bf16[2,64,1024]{2,1,0:T(8,128)(2,1)S(1)}, bf16[2,64,1024]{2,1,0:T(8,128)(2,1)}, u32[]{:S(2)}) copy-start(bf16[2,64,1024]{2,1,0:T(8,128)(2,1)} %get-tuple-element.278) | copy-start | bytes 786436
  288.1 62.6 %all-to-all-start = ((bf16[1,2,1024,1024]{3,1,0,2:T(2,128)(2,1)}), bf16[1,2,1024,1024]{3,1,0,2:T(2,128)(2,1)}, u32[]{:S(2)}, u32[]{:S(2)}) async-start(bf16[1,2,1024,1024]{3,1,0,2:T(2,128)(2,1)} %copy.101), calls=%async_computation | async-start | bytes 8388608 | tf_op jit(solution)/shard_map/all_to_all | solution.py:143
  350.7 10.4 %copy-start = (bf16[2,64,2048]{2,1,0:T(8,128)(2,1)S(1)}, bf16[2,64,2048]{2,1,0:T(8,128)(2,1)}, u32[]{:S(2)}) copy-start(bf16[2,64,2048]{2,1,0:T(8,128)(2,1)} %param.11) | copy-start | bytes 1572868
  360.2 4.2 %copy-start.3 = (f32[2048]{0:T(1024)S(1)}, f32[2048]{0:T(1024)}, u32[]{:S(2)}) copy-start(f32[2048]{0:T(1024)} %param.15) | copy-start | bytes 24580
  360.2 4.2 %copy-start.4 = (f32[2048]{0:T(1024)S(1)}, f32[2048]{0:T(1024)}, u32[]{:S(2)}) copy-start(f32[2048]{0:T(1024)} %param.14) | copy-start | bytes 24580
Sparse Core Ops, SparseCore 0:
  42.9 78.2 all-gather.5
  128.9 38.5 all-gather.7
  169.1 37.3 all-gather.9
  208.6 37.4 all-gather.11
  247.7 37.9 all-gather.13
where the time goes:
time: 376 us; the launch traced here: 372 us
  local copies, waits for them, and re-layouts  94.5 us (25%)
  waiting for transfers between devices  91.1 us (24%)
  blocking collectives  66.9 us (18%)
  matrix products  38.6 us (10%)
  other arithmetic  36.6 us (10%)
  starting transfers between devices  22.5 us (6%)
  between operations  14.5 us (4%)
  loops' own time  7.53 us (2%)
    all_gather x1, waiting for transfers between devices, body(): lax.all_gather(qkv_cols, 'fsdp', axis=0, tiled=True)  78.4 us
    all_gather x1, blocking collectives, body(): lax.all_gather(w_qkv, 'dp', axis=1, tiled=True)  35.5 us
    all_gather x1, blocking collectives, body(): lax.all_gather(w_out, 'dp', axis=1, tiled=True)  31.3 us
    unnamed x32, local copies, waits for them, and re-layouts  20.5 us
    dot_general x5, matrix products, one_block(): jnp.einsum('nhk,khd->nhd', expo.astype(jnp.bfloat16), value_rows, preferr...  17.8 us
    div x2, local copies, waits for them, and re-layouts, body(): owner_sum / jnp.maximum(owner_total, 1.0)[:, :, None]  15.7 us
    mul x2, local copies, waits for them, and re-layouts, body(): normed_parts.astype(jnp.float32) * factor[..., None]  15.5 us
    reduce_sum x5, other arithmetic, one_block(): row_total = jnp.sum(expo, axis=2)  12.5 us
  transfers between devices with their start and end apart: 8, of which 3 were waited for; matrix products, arithmetic and copies ran while one was open for 42% of the time, Pallas kernels for 0%

commit v1 on v0

--- a/solution.py
+++ b/solution.py
@@ -68,7 +68,9 @@
     flat_rows = tokens.reshape(req_count * tok_count, width)
     qkv_cols, out_cols = (
         lax.all_gather(w_qkv, "dp", axis=1, tiled=True),
-        lax.all_gather(w_out, "dp", axis=1, tiled=True),
+        jnp.concatenate(
+            lax.all_to_all(jnp.stack([w_out] * lax.axis_size("dp")), "dp", 0, 0), axis=1
+        ),
     )
     left_rows = flat_rows
     qkv_sum = jnp.dot(

time: 376 us -> 372 us (0.989)
  blocking collectives: 66.9 us -> 35.5 us
  waiting for transfers between devices: 91.1 us -> 114 us
    all_gather x1 -> x0, blocking collectives: 31.3 us -> none  [body(): lax.all_gather(w_out, 'dp', axis=1, tiled=True)]
    all_gather x1, waiting for transfers between devices: 2.29 us -> 21.3 us  [body(): lax.all_gather(own_queries, 'fsdp', axis=1, tiled=True)]
    all_to_all x0 -> x1, starting transfers between devices: none -> 6.59 us  [body(): lax.all_to_all(jnp.stack([w_out] * lax.axis_size('dp')), 'dp', 0, 0)]
    all_to_all x1, starting transfers between devices: 10.5 us -> 5.27 us  [body(): lax.all_to_all(part_max, 'fsdp', split_axis=2, concat_axis=0, tiled=True)]
  transfers between devices with their start and end apart: 8 -> 9, of which waited for: 3 -> 4; matrix products, arithmetic and copies ran while one was open for 42% -> 43% of each run, Pallas kernels for 0% -> 0%
where the time goes in v1:
time: 372 us; the launch traced here: 367 us
  waiting for transfers between devices  114 us (31%)
  local copies, waits for them, and re-layouts  96.1 us (26%)
  matrix products  38.7 us (10%)
  other arithmetic  36.7 us (10%)
  blocking collectives  35.5 us (10%)
  starting transfers between devices  24.1 us (6%)
  between operations  14.5 us (4%)
  loops' own time  7.99 us (2%)
    all_gather x1, waiting for transfers between devices, body(): lax.all_gather(qkv_cols, 'fsdp', axis=0, tiled=True)  78.4 us
    all_gather x1, blocking collectives, body(): lax.all_gather(w_qkv, 'dp', axis=1, tiled=True)  35.5 us
    all_gather x1, waiting for transfers between devices, body(): lax.all_gather(own_queries, 'fsdp', axis=1, tiled=True)  21.3 us
    unnamed x32, local copies, waits for them, and re-layouts  20.5 us
    dot_general x5, matrix products, one_block(): jnp.einsum('nhk,khd->nhd', expo.astype(jnp.bfloat16), value_rows, preferr...  17.8 us
    div x2, local copies, waits for them, and re-layouts, body(): owner_sum / jnp.maximum(owner_total, 1.0)[:, :, None]  15.7 us
    mul x2, local copies, waits for them, and re-layouts, body(): normed_parts.astype(jnp.float32) * factor[..., None]  15.5 us
    reduce_sum x5, other arithmetic, one_block(): row_total = jnp.sum(expo, axis=2)  12.5 us
  transfers between devices with their start and end apart: 9, of which 4 were waited for; matrix products, arithmetic and copies ran while one was open for 43% of the time, Pallas kernels for 0%

profile of v1, /device:TPU:3, one launch (start us, length us, event | category | flops | bytes accessed | tf_op | source)
XLA Modules:
  0.0 367.4 jit_solution(4965477434477831754)
XLA Ops:
  7.2 35.5 %all_gather.18 = bf16[128,3072]{1,0:T(8,128)(2,1)} all-gather(bf16[128,384]{1,0:T(8,128)(2,1)} %param.12), channel_id=1, replica_groups=mesh['dp'=8,'fsdp'=16] {'dp'}, dimensions={1}, use_global_device_ids=true | all-gather | bytes 884736 | tf_op jit(solution)/shard_map/all_gather | solution.py:70
  42.8 78.4 %all-gather.6.cloned.1.call-done = bf16[2048,3072]{1,0:T(8,128)(2,1)} async-done(((bf16[128,3072]{1,0:T(8,128)(2,1)}), bf16[2048,3072]{1,0:T(8,128)(2,1)}) %all-gather.6.cloned.1.call-update) | async-done | bytes 12582928 | tf_op jit(solution)/shard_map/all_gather | solution.py:78
  121.2 6.6 %convolution_convert_fusion = bf16[128,3072]{1,0:T(8,128)(2,1)S(1)} fusion(bf16[128,2048]{1,0:T(8,128)(2,1)} %bitcast.183, bf16[2048,3072]{1,0:T(8,128)(2,1)} %all-gather.6.cloned.1.call-done), kind=kOutput, calls=%fused_computation.42 | convolution fusion | flops 1611005952 | bytes 13893632 | tf_op jit(solution)/shard_map/dot_general | solution.py:76
  130.8 6.6 %all-to-all-start.3 = ((bf16[8,64,256]{2,1,0:T(8,128)(2,1)}), bf16[8,64,256]{2,1,0:T(8,128)(2,1)S(1)}, u32[]{:S(2)}, u32[]{:S(2)}) async-start(bf16[8,64,256]{2,1,0:T(8,128)(2,1)} %stack.2), calls=%async_computation.3 | async-start | bytes 524288 | tf_op jit(solution)/shard_map/all_to_all | solution.py:72
  141.7 3.7 %all-to-all-done.3 = bf16[8,64,256]{2,1,0:T(8,128)(2,1)S(1)} async-done(((bf16[8,64,256]{2,1,0:T(8,128)(2,1)}), bf16[8,64,256]{2,1,0:T(8,128)(2,1)S(1)}, u32[]{:S(2)}, u32[]{:S(2)}) %all-to-all-start.3) | async-done | bytes 262176 | tf_op jit(solution)/shard_map/all_to_all | solution.py:72
  146.2 21.3 %all-gather.8.cloned.1.call-done = bf16[2,1024,1024]{2,1,0:T(8,128)(2,1)} async-done(((bf16[2,64,1024]{2,1,0:T(8,128)(2,1)}), bf16[2,1024,1024]{2,1,0:T(8,128)(2,1)}) %all-gather.8.cloned.1.call-update) | async-done | bytes 4194320 | tf_op jit(solution)/shard_map/all_gather | solution.py:125
  167.5 5.2 %copy.136 = bf16[256,8,8,128]{3,2,1,0:T(8,128)(2,1)} copy(bf16[256,8,8,128]{3,1,2,0:T(8,128)(2,1)} %bitcast.172) | data formatting | bytes 8388608
  172.7 54.6 %while.4 = (s32[]{:T(128)}, f32[4,512,8,128]{3,2,1,0:T(8,128)}, f32[4,512,8]{1,2,0:T(8,128)S(1)}, f32[4,512,8]{1,2,0:T(8,128)S(1)}, s32[4]{0:T(128)S(1)}, /*inde...) while((s32[]{:T(128)}, f32[4,512,8,128]{3,2,1,0:T(8,128)}, ...), condition=%wide.region_6.7_spmd.clone, body=%wide.region_3.6_spmd.clone.sunk | while | flops 1101783552 | bytes 37900532 | solution.py:51
  230.1 5.3 %all-to-all-start.2 = ((f32[16,1,1024]{2,1,0:T(1,128)}), f32[16,1,1024]{2,1,0:T(1,128)S(1)}, u32[]{:S(2)}, u32[]{:S(2)}) async-start(f32[16,1,1024]{2,1,0:T(1,128)} %reshape.394), calls=%async_computation.2 | async-start | bytes 131072 | tf_op jit(solution)/shard_map/all_to_all | solution.py:147
  238.2 9.3 %reshape.385 = f32[1,2,1024,1024]{3,2,1,0:T(8,128)} reshape(f32[4,512,8,128]{3,2,1,0:T(8,128)} %get-tuple-element.136) | data formatting | bytes 16777216 | tf_op jit(solution)/shard_map/reshape | solution.py:53
  247.8 6.4 %div.34 = f32[2048,8,128]{2,1,0:T(8,128)} broadcast(f32[2048,8]{1,0:T(8,128)S(1)} %copy.103), dimensions={0,1} | broadcast | bytes 8454144 | tf_op jit(solution)/shard_map/div | solution.py:141
  254.2 9.3 %div.35 = f32[1,2,1024,1024]{3,2,1,0:T(8,128)} reshape(f32[2048,8,128]{2,1,0:T(8,128)} %div.34) | data formatting | bytes 16777216 | tf_op jit(solution)/shard_map/div | solution.py:141
  263.5 5.7 %all-to-all-start.1 = ((f32[16,1,1024]{2,1,0:T(1,128)}), f32[16,1,1024]{2,1,0:T(1,128)S(1)}, u32[]{:S(2)}, u32[]{:S(2)}) async-start(f32[16,1,1024]{2,1,0:T(1,128)} %reshape.396), calls=%async_computation.1 | async-start | bytes 131072 | tf_op jit(solution)/shard_map/all_to_all | solution.py:148
  269.2 7.8 %divide_convert_fusion = bf16[1,2,1024,1024]{3,2,1,0:T(8,128)(2,1)S(1)} fusion(f32[1,2,1024,1024]{3,2,1,0:T(8,128)} %reshape.385, f32[1,2,1024,1024]{3,2,1,0:T(8,128)} %div.35), kind=kLoop, calls=%fused_computation.30 | loop fusion | flops 4194304 | bytes 20971520 | tf_op jit(solution)/shard_map/convert_element_type | solution.py:141
  277.0 6.2 %copy.104 = bf16[1,2,1024,1024]{3,1,0,2:T(2,128)(2,1)} copy(bf16[1,2,1024,1024]{3,2,1,0:T(8,128)(2,1)S(1)} %divide_convert_fusion) | data formatting | bytes 8388608 | tf_op jit(solution)/shard_map/convert_element_type | solution.py:141
  283.3 6.0 %all-to-all-start = ((bf16[1,2,1024,1024]{3,1,0,2:T(2,128)(2,1)}), bf16[1,2,1024,1024]{3,1,0,2:T(2,128)(2,1)}, u32[]{:S(2)}, u32[]{:S(2)}) async-start(bf16[1,2,1024,1024]{3,1,0,2:T(2,128)(2,1)} %copy.104), calls=%async_computation | async-start | bytes 8388608 | tf_op jit(solution)/shard_map/all_to_all | solution.py:145
  292.0 3.3 copy.141
  295.3 4.9 %fusion.22 = (f32[128,8]{0,1:T(8,128)S(1)}, f32[8,2048,128]{2,1,0:T(8,128)}) fusion(pred[128,2048]{0,1:T(8,128)(4,1)S(1)} %and_select_fusion, bf16[128,8,128]{2,1,0:T(8,128)(2,1)S(1)} %bitcast.194, bf16[2048,8,128]{2,1,0:T(8,128)(2,1)S(1)} %bitcast.173), kind=kOutput, calls=%fused_computation.31 | convolution fusion | flops 543161344 | bytes 13111296 | tf_op jit(solution)/shard_map/while/body/eval_jaxpr/nhd,khd->nhk/dot_general | solution.py:28
  300.2 4.5 %fusion.23 = f32[128,8]{0,1:T(8,128)S(1)} fusion(f32[8,2048,128]{2,1,0:T(8,128)} %get-tuple-element.280, f32[128,8]{0,1:T(8,128)S(1)} %get-tuple-element.279, pred[128,2048]{0,1:T(8,128)(4,1)S(1)} %and_select_fusion), kind=kLoop, calls=%fused_computation.32 | loop fusion | flops 10484736 | bytes 8658944 | tf_op jit(solution)/shard_map/while/body/eval_jaxpr/reduce_sum | solution.py:41
  308.0 5.7 %fusion.25 = f32[8,128,128]{2,1,0:T(8,128)S(1)} fusion(bf16[2048,8,128]{2,1,0:T(8,128)(2,1)S(1)} %bitcast.174, f32[8,2048,128]{2,1,0:T(8,128)} %get-tuple-element.280, f32[128,8]{0,1:T(8,128)S(1)} %get-tuple-element.279, pred[128,2048]{0,1:T(8,128)(4,1)S(1)} %and_select_fusion), kind=kOutput, calls=%fused_computation.34 | convolution fusion | flops 547356672 | bytes 13373440 | tf_op jit(solution)/shard_map/while/body/eval_jaxpr/nhk,khd->nhd/dot_general | solution.py:42
  321.2 4.5 %mul.121 = f32[16,2,64,8,128]{4,3,1,2,0:T(8,128)} broadcast(f32[16,2,64,8]{3,1,2,0:T(2,128)S(1)} %copy.112), dimensions={0,1,2,3} | broadcast | bytes 8454144 | tf_op jit(solution)/shard_map/mul | solution.py:170
  325.7 11.0 %mul.122 = f32[16,1,2,64,1024]{4,2,3,0,1:T(2,128)} reshape(f32[16,2,64,8,128]{4,3,1,2,0:T(8,128)} %mul.121) | data formatting | bytes 16777216 | tf_op jit(solution)/shard_map/mul | solution.py:170
  336.7 9.1 %all-to-all-done = bf16[1,2,1024,1024]{3,1,0,2:T(2,128)(2,1)} async-done(((bf16[1,2,1024,1024]{3,1,0,2:T(2,128)(2,1)}), bf16[1,2,1024,1024]{3,1,0,2:T(2,128)(2,1)}, u32[]{:S(2)}, u32[]{:S(2)}) %all-to-all-start) | async-done | bytes 4194336 | tf_op jit(solution)/shard_map/all_to_all | solution.py:145
  345.8 9.5 %fusion.21 = f32[2,64,1024]{2,0,1:T(2,128)S(1)} fusion(f32[16,1,2,64,1024]{4,2,3,0,1:T(2,128)} %mul.122, bf16[1,2,16,64,1024]{4,1,3,2,0:T(2,128)(2,1)} %bitcast.27), kind=kLoop, calls=%fused_computation.27 | loop fusion | flops 6160384 | bytes 13107200 | tf_op jit(solution)/shard_map/reduce_sum | solution.py:170
  (147 shorter events, 79.0 us)
Async XLA Ops:
  7.2 114.0 %all-gather.6.cloned.1.call-start = ((), (), s32[]{:S(2)}) async-start(), calls=%async_computation.4 | async-start | bytes 13369344 | tf_op jit(solution)/shard_map/all_gather | solution.py:78
  42.8 124.7 %all-gather.8.cloned.1.call-start = ((), (), s32[]{:S(2)}) async-start(), calls=%async_computation.5 | async-start | bytes 4456448 | tf_op jit(solution)/shard_map/all_gather | solution.py:125
  121.2 8.8 %copy-start.2 = (bf16[64,256]{1,0:T(8,128)(2,1)S(1)}, bf16[64,256]{1,0:T(8,128)(2,1)}, u32[]{:S(2)}) copy-start(bf16[64,256]{1,0:T(8,128)(2,1)} %param.13) | copy-start | bytes 98308
  121.2 16.5 %copy-start.6 = (s32[2]{0:T(128)S(1)}, s32[2]{0:T(128)}, u32[]{:S(2)}) copy-start(s32[2]{0:T(128)} %param.19) | copy-start | bytes 28
  121.2 16.5 %copy-start.7 = (s32[4]{0:T(128)S(1)}, s32[4]{0:T(128)}, u32[]{:S(2)}) copy-start(s32[4]{0:T(128)} %param.18) | copy-start | bytes 52
  121.2 16.7 %copy-start.5 = (s32[4,16]{1,0:T(4,128)S(1)}, s32[4,16]{1,0:T(4,128)}, u32[]{:S(2)}) copy-start(s32[4,16]{1,0:T(4,128)} %param.17) | copy-start | bytes 772
  128.7 163.2 %all-gather.10.cloned.1.call-start = ((), (), s32[]{:S(2)}) async-start(), calls=%async_computation.6 | async-start | bytes 4456448 | tf_op jit(solution)/shard_map/all_gather | solution.py:126
  129.5 175.3 %all-gather.12.cloned.1.call-start = ((), (), s32[]{:S(2)}) async-start(), calls=%async_computation.7 | async-start | bytes 4456448 | tf_op jit(solution)/shard_map/all_gather | solution.py:127
  130.8 14.6 %all-to-all-start.3 = ((bf16[8,64,256]{2,1,0:T(8,128)(2,1)}), bf16[8,64,256]{2,1,0:T(8,128)(2,1)S(1)}, u32[]{:S(2)}, u32[]{:S(2)}) async-start(bf16[8,64,256]{2,1,0:T(8,128)(2,1)} %stack.2), calls=%async_computation.3 | async-start | bytes 524288 | tf_op jit(solution)/shard_map/all_to_all | solution.py:72
  137.4 218.9 %all-gather.14.cloned.1.call-start = ((), (), s32[]{:S(2)}) async-start(), calls=%async_computation.8 | async-start | bytes 4456448 | tf_op jit(solution)/shard_map/all_gather | solution.py:177
  230.1 33.4 %all-to-all-start.2 = ((f32[16,1,1024]{2,1,0:T(1,128)}), f32[16,1,1024]{2,1,0:T(1,128)S(1)}, u32[]{:S(2)}, u32[]{:S(2)}) async-start(f32[16,1,1024]{2,1,0:T(1,128)} %reshape.394), calls=%async_computation.2 | async-start | bytes 131072 | tf_op jit(solution)/shard_map/all_to_all | solution.py:147
  263.5 19.8 %all-to-all-start.1 = ((f32[16,1,1024]{2,1,0:T(1,128)}), f32[16,1,1024]{2,1,0:T(1,128)S(1)}, u32[]{:S(2)}, u32[]{:S(2)}) async-start(f32[16,1,1024]{2,1,0:T(1,128)} %reshape.396), calls=%async_computation.1 | async-start | bytes 131072 | tf_op jit(solution)/shard_map/all_to_all | solution.py:148
  277.0 14.9 %copy-start.1 = (bf16[2,64,1024]{2,1,0:T(8,128)(2,1)S(1)}, bf16[2,64,1024]{2,1,0:T(8,128)(2,1)}, u32[]{:S(2)}) copy-start(bf16[2,64,1024]{2,1,0:T(8,128)(2,1)} %get-tuple-element.278) | copy-start | bytes 786436
  283.3 62.5 %all-to-all-start = ((bf16[1,2,1024,1024]{3,1,0,2:T(2,128)(2,1)}), bf16[1,2,1024,1024]{3,1,0,2:T(2,128)(2,1)}, u32[]{:S(2)}, u32[]{:S(2)}) async-start(bf16[1,2,1024,1024]{3,1,0,2:T(2,128)(2,1)} %copy.104), calls=%async_computation | async-start | bytes 8388608 | tf_op jit(solution)/shard_map/all_to_all | solution.py:145
  345.8 10.4 %copy-start = (bf16[2,64,2048]{2,1,0:T(8,128)(2,1)S(1)}, bf16[2,64,2048]{2,1,0:T(8,128)(2,1)}, u32[]{:S(2)}) copy-start(bf16[2,64,2048]{2,1,0:T(8,128)(2,1)} %param.11) | copy-start | bytes 1572868
  355.4 4.2 %copy-start.3 = (f32[2048]{0:T(1024)S(1)}, f32[2048]{0:T(1024)}, u32[]{:S(2)}) copy-start(f32[2048]{0:T(1024)} %param.15) | copy-start | bytes 24580
  355.4 4.2 %copy-start.4 = (f32[2048]{0:T(1024)S(1)}, f32[2048]{0:T(1024)}, u32[]{:S(2)}) copy-start(f32[2048]{0:T(1024)} %param.14) | copy-start | bytes 24580
Sparse Core Ops, SparseCore 0:
  42.9 78.2 all-gather.5
  128.8 38.5 all-gather.7
  169.1 38.0 all-gather.9
  209.3 37.9 all-gather.11
  248.8 37.8 all-gather.13
